TPU v7x, 256 devices: a whole 4x4x8 slice. The times are simulated.
256 devices in a mesh: rows: 8 (over z), cols: 32 (over y, x, core).
Axes of the slice: x: 4, y: 4, z: 8, core: 2. Of those that a mesh axis runs over, the one named last changes fastest.
Arguments:
- whitened: float32 [3, 1048576], P(None, ('rows', 'cols')), may hold values from -6 to 6
- cotangent: bfloat16 [64, 1048576], P(None, ('rows', 'cols')), may hold values from -6 to 6
- lift_weight: float32 [64, 3], replicated, may hold values from -3.5 to 3.5
- conv_now: bfloat16 [3, 128, 64], replicated, may hold values from -0.5 to 0.5
- conv_past: bfloat16 [3, 128, 64], replicated, may hold values from -0.5 to 0.5
- mix_weight: bfloat16 [3, 64, 64], replicated, may hold values from -0.75 to 0.75
- dilations: int32 [3], replicated, may hold values from 64 to 256, as said below
- psd_bin: int32 [4096, 32, 8], P(None, 'cols', 'rows'), may hold values from 0 to 1023, as said below
- psd_weight: float32 [2, 1024], replicated, may hold values from 0.2 to 5
Outputs:
- data_grad: float32 [3, 1048576], P(None, ('rows', 'cols'))
- grad_now: float32 [3, 128, 64], replicated
- grad_past: float32 [3, 128, 64], replicated
- grad_mix: float32 [3, 64, 64], replicated
- grad_lift: float32 [64, 3], replicated
Inputs may be any that keep to these rules, and one draw needn't show every extreme that they name: `dilations`: multiples of 4; one layer has 64, one has 256. `psd_bin`: frequencies k and 1048576 - k have the same bin.
All inputs are finite; a program needn't handle non-finite values.
Results may differ from a plain program's by a relative error of at most 0.0068.
Values may be sent and summed in bfloat16 or wider, within the bound.
No kernel may reach another device: no remote copies, remote signals or barrier semaphores. Data moves between devices by JAX's collectives and lax.ppermute only.
A program may use at most 64 MiB of HBM per device.

v0:
```python
import math
import jax
import jax.numpy as jnp
from jax import lax
from jax.sharding import PartitionSpec as P

DMAX = 256


def from_behind(array, axis, by):
    peers = lax.axis_size(axis)
    pairs = [(i, i + by) for i in range(peers) if 0 <= i + by < peers]
    return lax.ppermute(array, axis, pairs)


def lifted(lift_weight, inputs):
    return (
        lift_weight[:, 0:1] * inputs[0:1]
        + lift_weight[:, 1:2] * inputs[1:2]
        + lift_weight[:, 2:3] * inputs[2:3]
    )


def delayed(field_b, delay, before):
    joined = jnp.concatenate([before, field_b], axis=1)
    start_at = before.shape[1] - delay
    return lax.dynamic_slice_in_dim(joined, start_at, field_b.shape[1], 1)


def advanced(values, delay, head_rim):
    joined = jnp.concatenate([values, head_rim], axis=1)
    return lax.dynamic_slice_in_dim(joined, delay, values.shape[1], 1)


def gated_layer(field_now, field_b, before, weight_now, weight_past, weight_mix, delay):
    channel_count = weight_mix.shape[0]
    past_b = delayed(field_b, delay, before)
    pre_act = jnp.dot(weight_now, field_b, preferred_element_type=jnp.float32) + jnp.dot(
        weight_past, past_b, preferred_element_type=jnp.float32
    )
    tanh_part = jnp.tanh(pre_act[:channel_count])
    sigm_part = jax.nn.sigmoid(pre_act[channel_count:])
    gate_b = (tanh_part * sigm_part).astype(jnp.bfloat16)
    field_next = field_now + jnp.dot(weight_mix, gate_b, preferred_element_type=jnp.float32)
    return (field_next, (field_b, past_b, tanh_part, sigm_part, gate_b))


def phase_angle(product, modulus, sign_factor):
    return sign_factor * 2.0 * math.pi / modulus * (product % modulus).astype(jnp.float32)


def phase_table(modulus, sign_factor):
    ordinal = jnp.arange(modulus, dtype=jnp.int32)
    angles = phase_angle(ordinal[:, None] * ordinal[None, :], modulus, sign_factor)
    return (jnp.cos(angles), jnp.sin(angles))


def rotate(signals, angles):
    real_part, imag_part = signals
    cosine = jnp.cos(angles)
    sine_part = jnp.sin(angles)
    return (real_part * cosine - imag_part * sine_part, real_part * sine_part + imag_part * cosine)


def transform(pattern, table_pair, signals):
    cosine, sine_part = table_pair
    real_part, imag_part = signals
    first_term = jnp.einsum(pattern, cosine, real_part, precision=lax.Precision.HIGHEST)
    second = jnp.einsum(pattern, sine_part, real_part, precision=lax.Precision.HIGHEST)
    if imag_part is None:
        return (first_term, second)
    return (
        first_term - jnp.einsum(pattern, sine_part, imag_part, precision=lax.Precision.HIGHEST),
        second + jnp.einsum(pattern, cosine, imag_part, precision=lax.Precision.HIGHEST),
    )


def split_length(length_all):
    chosen = 1
    for factor in range(1, length_all + 1):
        if length_all % factor == 0 and factor * factor <= length_all:
            chosen = factor
    return (chosen, length_all // chosen)


def pair_up(moved):
    return ((moved, None), (0, 0, 1))


def local_section(signals, psd_bin, psd_weight, weight_rows):
    rows_count = lax.axis_size("rows")
    row_index = lax.axis_index("rows")
    col_index = lax.axis_index("cols")
    signal_count = len(weight_rows)
    segment = signals[0].shape[1]
    length_all = segment * rows_count * lax.axis_size("cols")
    slow_len, fast_len = split_length(segment)
    slow_ids = jnp.arange(slow_len, dtype=jnp.int32)
    fast_ids = jnp.arange(fast_len, dtype=jnp.int32)
    spectra = (
        signals[0].reshape(signal_count, slow_len, fast_len),
        signals[1].reshape(signal_count, slow_len, fast_len),
    )
    spectra = transform("pa,kpq->kaq", phase_table(slow_len, -1.0), spectra)
    spectra = rotate(
        spectra, phase_angle(slow_ids[:, None] * fast_ids[None, :], segment, -1.0)[None]
    )
    spectra = transform("qb,kaq->kab", phase_table(fast_len, -1.0), spectra)
    bins_here = psd_bin.reshape(fast_len, slow_len).T
    weights = jnp.take(psd_weight, bins_here, axis=1)
    factors = jnp.stack([weights[row_id] for row_id in weight_rows])
    spectra = (spectra[0] * factors, spectra[1] * factors)
    spectra = transform("bq,kab->kaq", phase_table(fast_len, 1.0), spectra)
    spectra = rotate(
        spectra, phase_angle(slow_ids[:, None] * fast_ids[None, :], segment, 1.0)[None]
    )
    spectra = transform("ap,kaq->kpq", phase_table(slow_len, 1.0), spectra)
    low_here = row_index + rows_count * col_index
    sample_all = jnp.arange(segment, dtype=jnp.int32)
    return rotate(
        (spectra[0].reshape(signal_count, segment), spectra[1].reshape(signal_count, segment)),
        phase_angle(sample_all * low_here, length_all, 1.0)[None],
    )


def per_axis_filter(signal, psd_bin, psd_weight):
    rows_count = lax.axis_size("rows")
    cols_count = lax.axis_size("cols")
    row_index = lax.axis_index("rows")
    col_index = lax.axis_index("cols")
    segment = signal.shape[1]
    groups = rows_count * cols_count
    length_all = segment * groups
    piece_len = segment // rows_count
    small_len = segment // groups
    outer_ids = jnp.arange(rows_count, dtype=jnp.int32)
    inner_ids = jnp.arange(cols_count, dtype=jnp.int32)
    moved = lax.all_to_all(
        signal.reshape(3, 1, segment), "rows", split_axis=2, concat_axis=1, tiled=True
    )
    signals, weight_rows = pair_up(moved)
    signal_count = len(weight_rows)
    signals = transform("ra,krj->kaj", phase_table(rows_count, -1.0), signals)
    signals = rotate(signals, phase_angle(col_index * outer_ids, groups, -1.0)[None, :, None])
    pieces = (
        lax.all_to_all(
            signals[0].reshape(signal_count, rows_count, 1, piece_len),
            "cols",
            split_axis=3,
            concat_axis=2,
            tiled=True,
        ),
        lax.all_to_all(
            signals[1].reshape(signal_count, rows_count, 1, piece_len),
            "cols",
            split_axis=3,
            concat_axis=2,
            tiled=True,
        ),
    )
    turned = transform("cb,kacm->kabm", phase_table(cols_count, -1.0), (pieces[0], pieces[1]))
    freq_low = outer_ids[:, None, None] + rows_count * inner_ids[None, :, None]
    sample_at = (
        row_index * piece_len
        + col_index * small_len
        + jnp.arange(small_len, dtype=jnp.int32)[None, None, :]
    )
    turned = rotate(turned, phase_angle(sample_at * freq_low, length_all, -1.0)[None])
    signals = (
        lax.all_to_all(turned[0], "cols", split_axis=2, concat_axis=3, tiled=True),
        lax.all_to_all(turned[1], "cols", split_axis=2, concat_axis=3, tiled=True),
    )
    signals = (
        lax.all_to_all(
            signals[0].reshape(signal_count, rows_count, piece_len),
            "rows",
            split_axis=1,
            concat_axis=2,
            tiled=True,
        ),
        lax.all_to_all(
            signals[1].reshape(signal_count, rows_count, piece_len),
            "rows",
            split_axis=1,
            concat_axis=2,
            tiled=True,
        ),
    )
    flat = local_section(
        (signals[0].reshape(signal_count, segment), signals[1].reshape(signal_count, segment)),
        psd_bin,
        psd_weight,
        weight_rows,
    )
    returned = (
        lax.all_to_all(
            flat[0].reshape(signal_count, 1, segment),
            "rows",
            split_axis=2,
            concat_axis=1,
            tiled=True,
        ),
        lax.all_to_all(
            flat[1].reshape(signal_count, 1, segment),
            "rows",
            split_axis=2,
            concat_axis=1,
            tiled=True,
        ),
    )
    pieces = (
        lax.all_to_all(
            returned[0].reshape(signal_count, rows_count, 1, piece_len),
            "cols",
            split_axis=3,
            concat_axis=2,
            tiled=True,
        ),
        lax.all_to_all(
            returned[1].reshape(signal_count, rows_count, 1, piece_len),
            "cols",
            split_axis=3,
            concat_axis=2,
            tiled=True,
        ),
    )
    turned = transform("bc,kabm->kacm", phase_table(cols_count, 1.0), (pieces[0], pieces[1]))
    turned = rotate(
        turned, phase_angle(inner_ids[None, :, None] * outer_ids[:, None, None], groups, 1.0)[None]
    )
    returned = (
        lax.all_to_all(turned[0], "cols", split_axis=2, concat_axis=3, tiled=True),
        lax.all_to_all(turned[1], "cols", split_axis=2, concat_axis=3, tiled=True),
    )
    real_in = returned[0].reshape(signal_count, rows_count, piece_len)
    imag_in = returned[1].reshape(signal_count, rows_count, piece_len)
    cos_rows, sin_rows = phase_table(rows_count, 1.0)
    real_out = jnp.einsum(
        "ar,kaj->krj", cos_rows, real_in, precision=lax.Precision.HIGHEST
    ) - jnp.einsum("ar,kaj->krj", sin_rows, imag_in, precision=lax.Precision.HIGHEST)
    homed = lax.all_to_all(real_out, "rows", split_axis=1, concat_axis=2, tiled=True)
    return homed.reshape(3, segment) / float(length_all)


def local(
    whitened,
    cotangent,
    lift_weight,
    conv_now,
    conv_past,
    mix_weight,
    dilations,
    psd_bin,
    psd_weight,
):
    segment = whitened.shape[1]
    layer_count = mix_weight.shape[0]
    saved = []
    field_now = lifted(lift_weight, whitened)
    for layer_id in range(layer_count):
        field_b = field_now.astype(jnp.bfloat16)
        before = from_behind(field_b[:, segment - DMAX :], ("rows", "cols"), 1)
        field_now, kept_parts = gated_layer(
            field_now,
            field_b,
            before,
            conv_now[layer_id],
            conv_past[layer_id],
            mix_weight[layer_id],
            dilations[layer_id],
        )
        saved.append(kept_parts)
    grad_field = cotangent.astype(jnp.float32)
    grads_now = [None] * layer_count
    grads_past = [None] * layer_count
    grads_mix = [None] * layer_count
    for layer_id in reversed(range(layer_count)):
        field_b, past_b, tanh_part, sigm_part, gate_b = saved[layer_id]
        grad_field_b = grad_field.astype(jnp.bfloat16)
        grad_gate = jnp.dot(
            mix_weight[layer_id].T, grad_field_b, preferred_element_type=jnp.float32
        )
        grads_mix[layer_id] = jnp.dot(grad_field_b, gate_b.T, preferred_element_type=jnp.float32)
        grad_pre = jnp.concatenate(
            [
                grad_gate * sigm_part * (1.0 - tanh_part * tanh_part),
                grad_gate * tanh_part * sigm_part * (1.0 - sigm_part),
            ],
            axis=0,
        ).astype(jnp.bfloat16)
        grads_now[layer_id] = jnp.dot(grad_pre, field_b.T, preferred_element_type=jnp.float32)
        grads_past[layer_id] = jnp.dot(grad_pre, past_b.T, preferred_element_type=jnp.float32)
        ahead_term = jnp.dot(conv_past[layer_id].T, grad_pre, preferred_element_type=jnp.float32)
        head_rim = from_behind(ahead_term[:, :DMAX], ("rows", "cols"), -1)
        grad_field = (
            grad_field
            + jnp.dot(conv_now[layer_id].T, grad_pre, preferred_element_type=jnp.float32)
            + advanced(ahead_term, dilations[layer_id], head_rim)
        )
    input_grad = jnp.dot(lift_weight.T, grad_field, precision=lax.Precision.HIGHEST)
    lift_part = jnp.dot(grad_field, whitened.T, precision=lax.Precision.HIGHEST)
    summed = lax.psum(
        (jnp.stack(grads_now), jnp.stack(grads_past), jnp.stack(grads_mix), lift_part),
        ("rows", "cols"),
    )
    scaling = 1.0 / math.sqrt(float(segment * lax.axis_size("rows") * lax.axis_size("cols")))
    data_grad = per_axis_filter(input_grad, psd_bin, psd_weight)
    return (
        data_grad,
        summed[0] * scaling,
        summed[1] * scaling,
        summed[2] * scaling,
        summed[3] * scaling,
    )


def solution(mesh):
    in_specs = (
        P(None, ("rows", "cols")),
        P(None, ("rows", "cols")),
        P(),
        P(),
        P(),
        P(),
        P(),
        P(None, "cols", "rows"),
        P(),
    )
    out_specs = (P(None, ("rows", "cols")), P(), P(), P(), P())
    return jax.shard_map(local, mesh=mesh, in_specs=in_specs, out_specs=out_specs, check_vma=False)
```

profile of v0, /device:TPU:1, one launch (start us, length us, event | category | flops | bytes accessed | tf_op | source)
XLA Modules:
  0.0 555.5 jit_solution(1703089150025152943)
XLA Ops:
  9.3 4.6 collective-permute-start
  21.3 10.8 %gather_fusion = f32[4096,2]{1,0:T(8,128)S(1)} fusion(f32[2,1024]{0,1:T(8,128)S(1)} %copy.178, s32[4096]{0:T(1024)S(1)} %broadcast_clamp_fusion), kind=kCustom, calls=%fused_computation | custom fusion | bytes 81920 | tf_op jit(solution)/shard_map/jit(_take)/gather | solution.py:110
  87.3 20.4 %reduce.4 = f32[4096,3]{1,0:T(8,128)} reduce(f32[4096,1,3]{2,1,0:T(1,128)} %bitcast.335, f32[]{:T(128)} %broadcast.734), dimensions={1}, to_apply=%bitcast.265.reduce_sub_computation | reduce | bytes 98308
  111.4 21.0 %all-to-all-start = ((f32[8,1,1536]{2,1,0:T(1,128)}), f32[8,1,1536]{2,1,0:T(1,128)S(1)}, u32[]{:S(2)}, u32[]{:S(2)}) async-start(f32[8,1,1536]{2,1,0:T(1,128)} %reshape.486), calls=%async_computation | async-start | bytes 98304 | tf_op jit(solution)/shard_map/all_to_all | solution.py:138
  134.4 5.1 all-to-all-done
  140.3 4.4 reshape.487
  156.7 14.5 %all-to-all-start.1 = ((f32[32,1,384]{2,1,0:T(1,128)}), f32[32,1,384]{2,1,0:T(1,128)S(1)}, u32[]{:S(2)}, u32[]{:S(2)}) async-start(f32[32,1,384]{2,1,0:T(1,128)} %reshape.488), calls=%async_computation.1 | async-start | bytes 98304 | tf_op jit(solution)/shard_map/all_to_all | solution.py:146
  180.5 7.9 %all-to-all-start.2 = ((f32[32,1,384]{2,1,0:T(1,128)}), f32[32,1,384]{2,1,0:T(1,128)S(1)}, u32[]{:S(2)}, u32[]{:S(2)}) async-start(f32[32,1,384]{2,1,0:T(1,128)} %reshape.490), calls=%async_computation.2 | async-start | bytes 98304 | tf_op jit(solution)/shard_map/all_to_all | solution.py:153
  206.4 6.2 %all-to-all-start.3 = ((f32[32,1,384]{2,1,0:T(1,128)}), f32[32,1,384]{2,1,0:T(1,128)}, u32[]{:S(2)}, u32[]{:S(2)}) async-start(f32[32,1,384]{2,1,0:T(1,128)} %reshape.492), calls=%async_computation.3 | async-start | bytes 98304 | tf_op jit(solution)/shard_map/all_to_all | solution.py:170
  220.0 4.5 all-to-all-start.5
  242.4 4.5 all-to-all-start.6
  247.8 6.3 %all-to-all-done.6 = f32[3,8,512]{2,0,1:T(4,128)S(1)} async-done(((f32[3,8,512]{2,0,1:T(4,128)}), f32[3,8,512]{2,0,1:T(4,128)S(1)}, u32[]{:S(2)}, u32[]{:S(2)}) %all-to-all-start.6) | async-done | bytes 49184 | tf_op jit(solution)/shard_map/all_to_all | solution.py:181
  262.5 19.4 %reduce.12 = f32[4096,3]{1,0:T(8,128)} reduce(f32[4096,1,3]{2,1,0:T(1,128)S(1)} %bitcast.337, f32[]{:T(128)} %broadcast.734), dimensions={1}, to_apply=%bitcast.275.reduce_sub_computation | reduce | bytes 98308
  292.4 19.4 %reduce.16 = f32[4096,3]{1,0:T(8,128)} reduce(f32[4096,1,3]{2,1,0:T(1,128)S(1)} %bitcast.338, f32[]{:T(128)} %broadcast.734), dimensions={1}, to_apply=%bitcast.279.reduce_sub_computation | reduce | bytes 98308
  315.5 6.8 %all-to-all-start.9 = ((f32[8,1,1536]{2,1,0:T(1,128)}), f32[8,1,1536]{2,1,0:T(1,128)S(1)}, u32[]{:S(2)}, u32[]{:S(2)}) async-start(f32[8,1,1536]{2,1,0:T(1,128)} %reshape.500), calls=%async_computation.9 | async-start | bytes 98304 | tf_op jit(solution)/shard_map/all_to_all | solution.py:203
  326.2 4.3 copy.190
  335.7 6.2 %all-to-all-start.8 = ((f32[32,1,384]{2,1,0:T(1,128)}), f32[32,1,384]{2,1,0:T(1,128)S(1)}, u32[]{:S(2)}, u32[]{:S(2)}) async-start(f32[32,1,384]{2,1,0:T(1,128)} %reshape.498), calls=%async_computation.8 | async-start | bytes 98304 | tf_op jit(solution)/shard_map/all_to_all | solution.py:212
  342.8 79.2 %all-reduce = (f32[3,64,64]{2,1,0:T(8,128)S(1)}, f32[64,3]{0,1:T(4,128)S(1)}) all-reduce(f32[3,64,64]{2,1,0:T(8,128)S(1)} %pad_maximum_fusion.6, f32[64,3]{0,1:T(4,128)S(1)} %fusion.359), channel_id=1, replica_groups=mesh['rows'=8,'cols'=32] {'rows','cols'}, use_global_device_ids=true, to_apply=%region_2.0 | all-reduce | flops 12480 | bytes 99840 | tf_op jit(solution)/shard_map/psum | solution.py:302
  434.2 4.7 all-to-all-start.10
  451.9 4.8 all-to-all-start.12
  458.4 5.6 %all-to-all-done.12 = f32[32,1,384]{2,1,0:T(1,128)S(1)} async-done(((f32[32,1,384]{2,1,0:T(1,128)}), f32[32,1,384]{2,1,0:T(1,128)S(1)}, u32[]{:S(2)}, u32[]{:S(2)}) %all-to-all-start.12) | async-done | bytes 49184 | tf_op jit(solution)/shard_map/all_to_all | solution.py:233
  469.7 5.6 %all-to-all-done.11 = f32[32,1,384]{2,1,0:T(1,128)S(1)} async-done(((f32[32,1,384]{2,1,0:T(1,128)}), f32[32,1,384]{2,1,0:T(1,128)S(1)}, u32[]{:S(2)}, u32[]{:S(2)}) %all-to-all-start.11) | async-done | bytes 49184 | tf_op jit(solution)/shard_map/all_to_all | solution.py:232
  477.7 5.1 all-to-all-start.13
  482.8 63.4 %all-reduce.4.cloned.1.call-done = (f32[3,128,64]{1,2,0:T(8,128)}, f32[3,128,64]{1,2,0:T(8,128)}) async-done(((f32[3,128,64]{1,2,0:T(8,128)}, f32[3,128,64]{1,2,0:T(8,128)}), (f32[3,128,64]{1,2,0:T(8,128)}, f32[3,128,64]{1,2,0:T(8,128)})) %all-reduce.4.cloned.1.call-update) | async-done | bytes 196624 | tf_op jit(solution)/shard_map/psum | solution.py:302
  (291 shorter events, 195.4 us)
Async XLA Ops:
  8.0 24.8 %copy-start.40 = (f32[64]{0:T(128)}, f32[64]{0:T(128)S(1)}, u32[]{:S(2)}) copy-start(f32[64]{0:T(128)S(1)} %get-tuple-element.30) | copy-start | bytes 772
  9.2 37.5 %copy-start.5 = (bf16[64,4096]{1,0:T(8,128)(2,1)}, bf16[64,4096]{1,0:T(8,128)(2,1)S(1)}, u32[]{:S(2)}) copy-start(bf16[64,4096]{1,0:T(8,128)(2,1)S(1)} %fusion.33) | copy-start | bytes 1572868
  9.3 37.5 %collective-permute-start = (bf16[64,256]{1,0:T(8,128)(2,1)S(1)}, bf16[64,256]{1,0:T(8,128)(2,1)S(1)}, u32[]{:S(2)}, u32[]{:S(2)}) collective-permute-start(bf16[64,256]{1,0:T(8,128)(2,1)S(1)} %slice.140), channel_id=1, source_target_pairs={{0,1},{1,2},{2,3},{3,4},{4,5},{5,6},{6,7},{7,8},{8,9},{9,10},{10,1... | collective-permute-start | bytes 98312 | tf_op jit(solution)/shard_map/ppermute | solution.py:13
  48.5 29.5 %copy-start = (bf16[64,4096]{1,0:T(8,128)(2,1)}, bf16[64,4096]{1,0:T(8,128)(2,1)S(1)}, u32[]{:S(2)}) copy-start(bf16[64,4096]{1,0:T(8,128)(2,1)S(1)} %get-tuple-element.34) | copy-start | bytes 1572868
  48.6 3.1 collective-permute-start.1
  53.0 5.1 collective-permute-start.2
  60.9 6.2 %collective-permute-start.3 = (f32[64,256]{1,0:T(8,128)S(1)}, f32[64,256]{1,0:T(8,128)S(1)}, u32[]{:S(2)}, u32[]{:S(2)}) collective-permute-start(f32[64,256]{1,0:T(8,128)S(1)} %slice.149), channel_id=1, source_target_pairs={{1,0},{2,1},{3,2},{4,3},{5,4},{6,5},{7,6},{8,7},{9,8},{10,9},{11,1... | collective-permute-start | bytes 196616 | tf_op jit(solution)/shard_map/ppermute | solution.py:13
  68.8 5.6 %collective-permute-start.4 = (f32[64,256]{1,0:T(8,128)S(1)}, f32[64,256]{1,0:T(8,128)S(1)}, u32[]{:S(2)}, u32[]{:S(2)}) collective-permute-start(f32[64,256]{1,0:T(8,128)S(1)} %slice.150), channel_id=1, source_target_pairs={{1,0},{2,1},{3,2},{4,3},{5,4},{6,5},{7,6},{8,7},{9,8},{10,9},{11,1... | collective-permute-start | bytes 196616 | tf_op jit(solution)/shard_map/ppermute | solution.py:13
  76.1 5.6 %collective-permute-start.5 = (f32[64,256]{1,0:T(8,128)S(1)}, f32[64,256]{1,0:T(8,128)S(1)}, u32[]{:S(2)}, u32[]{:S(2)}) collective-permute-start(f32[64,256]{1,0:T(8,128)S(1)} %slice.151), channel_id=1, source_target_pairs={{1,0},{2,1},{3,2},{4,3},{5,4},{6,5},{7,6},{8,7},{9,8},{10,9},{11,1... | collective-permute-start | bytes 196616 | tf_op jit(solution)/shard_map/ppermute | solution.py:13
  111.4 28.1 %all-to-all-start = ((f32[8,1,1536]{2,1,0:T(1,128)}), f32[8,1,1536]{2,1,0:T(1,128)S(1)}, u32[]{:S(2)}, u32[]{:S(2)}) async-start(f32[8,1,1536]{2,1,0:T(1,128)} %reshape.486), calls=%async_computation | async-start | bytes 98304 | tf_op jit(solution)/shard_map/all_to_all | solution.py:138
  156.7 23.8 %all-to-all-start.1 = ((f32[32,1,384]{2,1,0:T(1,128)}), f32[32,1,384]{2,1,0:T(1,128)S(1)}, u32[]{:S(2)}, u32[]{:S(2)}) async-start(f32[32,1,384]{2,1,0:T(1,128)} %reshape.488), calls=%async_computation.1 | async-start | bytes 98304 | tf_op jit(solution)/shard_map/all_to_all | solution.py:146
  180.5 15.1 %all-to-all-start.2 = ((f32[32,1,384]{2,1,0:T(1,128)}), f32[32,1,384]{2,1,0:T(1,128)S(1)}, u32[]{:S(2)}, u32[]{:S(2)}) async-start(f32[32,1,384]{2,1,0:T(1,128)} %reshape.490), calls=%async_computation.2 | async-start | bytes 98304 | tf_op jit(solution)/shard_map/all_to_all | solution.py:153
  206.4 13.6 %all-to-all-start.3 = ((f32[32,1,384]{2,1,0:T(1,128)}), f32[32,1,384]{2,1,0:T(1,128)}, u32[]{:S(2)}, u32[]{:S(2)}) async-start(f32[32,1,384]{2,1,0:T(1,128)} %reshape.492), calls=%async_computation.3 | async-start | bytes 98304 | tf_op jit(solution)/shard_map/all_to_all | solution.py:170
  220.0 12.0 %all-to-all-start.5 = ((f32[32,1,384]{2,1,0:T(1,128)}), f32[32,1,384]{2,1,0:T(1,128)}, u32[]{:S(2)}, u32[]{:S(2)}) async-start(f32[32,1,384]{2,1,0:T(1,128)} %reshape.494), calls=%async_computation.5 | async-start | bytes 98304 | tf_op jit(solution)/shard_map/all_to_all | solution.py:171
  232.0 10.4 %all-to-all-start.4 = ((f32[3,8,512]{2,0,1:T(4,128)}), f32[3,8,512]{2,0,1:T(4,128)S(1)}, u32[]{:S(2)}, u32[]{:S(2)}) async-start(f32[3,8,512]{2,0,1:T(4,128)} %reshape.475), calls=%async_computation.4 | async-start | bytes 131072 | tf_op jit(solution)/shard_map/all_to_all | solution.py:174
  242.4 11.7 %all-to-all-start.6 = ((f32[3,8,512]{2,0,1:T(4,128)}), f32[3,8,512]{2,0,1:T(4,128)S(1)}, u32[]{:S(2)}, u32[]{:S(2)}) async-start(f32[3,8,512]{2,0,1:T(4,128)} %reshape.476), calls=%async_computation.6 | async-start | bytes 131072 | tf_op jit(solution)/shard_map/all_to_all | solution.py:181
  285.6 29.9 %all-to-all-start.7 = ((f32[8,1,1536]{2,1,0:T(1,128)}), f32[8,1,1536]{2,1,0:T(1,128)S(1)}, u32[]{:S(2)}, u32[]{:S(2)}) async-start(f32[8,1,1536]{2,1,0:T(1,128)} %reshape.496), calls=%async_computation.7 | async-start | bytes 98304 | tf_op jit(solution)/shard_map/all_to_all | solution.py:196
  289.0 257.3 %all-reduce.4.cloned.1.call-start = ((), (), s32[]{:S(2)}) async-start(), calls=%async_computation.14 | async-start | bytes 393216 | tf_op jit(solution)/shard_map/psum | solution.py:302
  315.5 20.2 %all-to-all-start.9 = ((f32[8,1,1536]{2,1,0:T(1,128)}), f32[8,1,1536]{2,1,0:T(1,128)S(1)}, u32[]{:S(2)}, u32[]{:S(2)}) async-start(f32[8,1,1536]{2,1,0:T(1,128)} %reshape.500), calls=%async_computation.9 | async-start | bytes 98304 | tf_op jit(solution)/shard_map/all_to_all | solution.py:203
  335.7 98.6 %all-to-all-start.8 = ((f32[32,1,384]{2,1,0:T(1,128)}), f32[32,1,384]{2,1,0:T(1,128)S(1)}, u32[]{:S(2)}, u32[]{:S(2)}) async-start(f32[32,1,384]{2,1,0:T(1,128)} %reshape.498), calls=%async_computation.8 | async-start | bytes 98304 | tf_op jit(solution)/shard_map/all_to_all | solution.py:212
  434.2 12.0 %all-to-all-start.10 = ((f32[32,1,384]{2,1,0:T(1,128)}), f32[32,1,384]{2,1,0:T(1,128)S(1)}, u32[]{:S(2)}, u32[]{:S(2)}) async-start(f32[32,1,384]{2,1,0:T(1,128)} %reshape.502), calls=%async_computation.10 | async-start | bytes 98304 | tf_op jit(solution)/shard_map/all_to_all | solution.py:219
  451.9 12.1 %all-to-all-start.12 = ((f32[32,1,384]{2,1,0:T(1,128)}), f32[32,1,384]{2,1,0:T(1,128)S(1)}, u32[]{:S(2)}, u32[]{:S(2)}) async-start(f32[32,1,384]{2,1,0:T(1,128)} %reshape.506), calls=%async_computation.12 | async-start | bytes 98304 | tf_op jit(solution)/shard_map/all_to_all | solution.py:233
  464.0 11.3 %all-to-all-start.11 = ((f32[32,1,384]{2,1,0:T(1,128)}), f32[32,1,384]{2,1,0:T(1,128)S(1)}, u32[]{:S(2)}, u32[]{:S(2)}) async-start(f32[32,1,384]{2,1,0:T(1,128)} %reshape.504), calls=%async_computation.11 | async-start | bytes 98304 | tf_op jit(solution)/shard_map/all_to_all | solution.py:232
  477.7 70.2 %all-to-all-start.13 = ((f32[3,8,512]{2,0,1:T(4,128)}), f32[3,8,512]{2,0,1:T(4,128)S(1)}, u32[]{:S(2)}, u32[]{:S(2)}) async-start(f32[3,8,512]{2,0,1:T(4,128)} %copy.204), calls=%async_computation.13 | async-start | bytes 131072 | tf_op jit(solution)/shard_map/all_to_all | solution.py:241
  (43 other events, 436.5 us)
Sparse Core Ops, SparseCore 0:
  296.0 250.2 all-reduce.3
where the time goes:
time: 566 us; the launch traced here: 556 us
  starting transfers between devices  114 us (20%)
  waiting for transfers between devices  109 us (19%)
  other arithmetic  97.2 us (17%)
  local copies, waits for them, and re-layouts  90 us (16%)
  blocking collectives  79.2 us (14%)
  matrix products  40.8 us (7%)
  between operations  25.4 us (4%)
    psum x1, blocking collectives, local(): lax.psum((jnp.stack(grads_now), jnp.stack(grads_past), jnp.stack(grads_mi...  79.2 us
    unnamed x8, other arithmetic  76 us
    psum x1, waiting for transfers between devices, local(): lax.psum((jnp.stack(grads_now), jnp.stack(grads_past), jnp.stack(grads_mi...  63.4 us
    unnamed x117, local copies, waits for them, and re-layouts  39.2 us
    all_to_all x1, starting transfers between devices, per_axis_filter(): lax.all_to_all(signal.reshape(3, 1, segment), 'rows', split_axis=2, conca...  21 us
    ppermute x6, starting transfers between devices, from_behind(): return lax.ppermute(array, axis, pairs)  16.5 us
    all_to_all x1, starting transfers between devices, per_axis_filter(): lax.all_to_all(signals[0].reshape(signal_count, rows_count, 1, piece_len)...  14.5 us
    gather x2, local copies, waits for them, and re-layouts, local_section(): weights = jnp.take(psd_weight, bins_here, axis=1)  11.5 us
  transfers between devices with their start and end apart: 21, of which 15 were waited for; matrix products, arithmetic and copies ran while one was open for 23% of the time, Pallas kernels for 0%

commit v1 on v0

--- a/solution.py
+++ b/solution.py
@@ -300,8 +300,10 @@
     input_grad = jnp.dot(lift_weight.T, grad_field, precision=lax.Precision.HIGHEST)
     lift_part = jnp.dot(grad_field, whitened.T, precision=lax.Precision.HIGHEST)
     summed = lax.psum(
-        (jnp.stack(grads_now), jnp.stack(grads_past), jnp.stack(grads_mix), lift_part),
-        ("rows", "cols"),
+        lax.psum(
+            (jnp.stack(grads_now), jnp.stack(grads_past), jnp.stack(grads_mix), lift_part), "rows"
+        ),
+        "cols",
     )
     scaling = 1.0 / math.sqrt(float(segment * lax.axis_size("rows") * lax.axis_size("cols")))
     data_grad = per_axis_filter(input_grad, psd_bin, psd_weight)

time: 566 us -> 670 us (1.18)
  blocking collectives: 79.2 us -> 151 us
  waiting for transfers between devices: 109 us -> 150 us
    psum x0 -> x1, blocking collectives: none -> 126 us  [local(): lax.psum(lax.psum((jnp.stack(grads_now), jnp.stack(grads_past), jnp.stack...]
    psum x0 -> x1, waiting for transfers between devices: none -> 99.3 us  [local(): lax.psum(lax.psum((jnp.stack(grads_now), jnp.stack(grads_past), jnp.stack...]
    psum x1, waiting for transfers between devices: 63.4 us -> 0.01 us  [local(): lax.psum((jnp.stack(grads_now), jnp.stack(grads_past), jnp.stack(grads_mi...]
    psum x1, blocking collectives: 79.2 us -> 24.9 us  [local(): lax.psum((jnp.stack(grads_now), jnp.stack(grads_past), jnp.stack(grads_mi...]
    unnamed x117 -> x101, local copies, waits for them, and re-layouts: 39.2 us -> 39.1 us
  transfers between devices with their start and end apart: 21 -> 22, of which waited for: 15 -> 16; matrix products, arithmetic and copies ran while one was open for 23% -> 22% of each run, Pallas kernels for 0% -> 0%
where the time goes in v1:
time: 670 us; the launch traced here: 660 us
  blocking collectives  151 us (23%)
  waiting for transfers between devices  150 us (22%)
  starting transfers between devices  114 us (17%)
  other arithmetic  95.5 us (14%)
  local copies, waits for them, and re-layouts  86.5 us (13%)
  matrix products  37.6 us (6%)
  between operations  25.2 us (4%)
    psum x1, blocking collectives, local(): lax.psum(lax.psum((jnp.stack(grads_now), jnp.stack(grads_past), jnp.stack...  126 us
    psum x1, waiting for transfers between devices, local(): lax.psum(lax.psum((jnp.stack(grads_now), jnp.stack(grads_past), jnp.stack...  99.3 us
    unnamed x8, other arithmetic  74.8 us
    unnamed x101, local copies, waits for them, and re-layouts  39.1 us
    psum x1, blocking collectives, local(): lax.psum((jnp.stack(grads_now), jnp.stack(grads_past), jnp.stack(grads_mi...  24.9 us
    all_to_all x1, starting transfers between devices, per_axis_filter(): lax.all_to_all(signal.reshape(3, 1, segment), 'rows', split_axis=2, conca...  21.1 us
    ppermute x6, starting transfers between devices, from_behind(): return lax.ppermute(array, axis, pairs)  16.4 us
    all_to_all x1, starting transfers between devices, per_axis_filter(): lax.all_to_all(signals[0].reshape(signal_count, rows_count, 1, piece_len)...  14.5 us
  transfers between devices with their start and end apart: 22, of which 16 were waited for; matrix products, arithmetic and copies ran while one was open for 22% of the time, Pallas kernels for 0%

profile of v1, /device:TPU:1, one launch (start us, length us, event | category | flops | bytes accessed | tf_op | source)
XLA Modules:
  0.0 660.2 jit_solution(5185480509039228165)
XLA Ops:
  9.9 4.5 collective-permute-start
  22.4 10.8 %gather_fusion = f32[4096,2]{1,0:T(8,128)S(1)} fusion(f32[2,1024]{0,1:T(8,128)S(1)} %copy.178, s32[4096]{0:T(1024)S(1)} %broadcast_clamp_fusion), kind=kCustom, calls=%fused_computation | custom fusion | bytes 81920 | tf_op jit(solution)/shard_map/jit(_take)/gather | solution.py:110
  90.0 20.4 %reduce.4 = f32[4096,3]{1,0:T(8,128)} reduce(f32[4096,1,3]{2,1,0:T(1,128)} %bitcast.335, f32[]{:T(128)} %broadcast.734), dimensions={1}, to_apply=%bitcast.265.reduce_sub_computation | reduce | bytes 98308
  114.1 21.1 %all-to-all-start = ((f32[8,1,1536]{2,1,0:T(1,128)}), f32[8,1,1536]{2,1,0:T(1,128)S(1)}, u32[]{:S(2)}, u32[]{:S(2)}) async-start(f32[8,1,1536]{2,1,0:T(1,128)} %reshape.486), calls=%async_computation | async-start | bytes 98304 | tf_op jit(solution)/shard_map/all_to_all | solution.py:138
  137.4 4.8 all-to-all-done
  143.0 4.4 reshape.487
  152.8 4.3 reduce.6
  159.5 14.5 %all-to-all-start.1 = ((f32[32,1,384]{2,1,0:T(1,128)}), f32[32,1,384]{2,1,0:T(1,128)S(1)}, u32[]{:S(2)}, u32[]{:S(2)}) async-start(f32[32,1,384]{2,1,0:T(1,128)} %reshape.488), calls=%async_computation.1 | async-start | bytes 98304 | tf_op jit(solution)/shard_map/all_to_all | solution.py:146
  181.3 6.9 %all-to-all-start.2 = ((f32[32,1,384]{2,1,0:T(1,128)}), f32[32,1,384]{2,1,0:T(1,128)S(1)}, u32[]{:S(2)}, u32[]{:S(2)}) async-start(f32[32,1,384]{2,1,0:T(1,128)} %reshape.490), calls=%async_computation.2 | async-start | bytes 98304 | tf_op jit(solution)/shard_map/all_to_all | solution.py:153
  203.5 4.9 all-to-all-start.3
  210.8 4.8 all-to-all-done.3
  233.1 4.3 all-to-all-done.4
  241.8 6.3 all-to-all-done.6
  256.5 19.4 %reduce.12 = f32[4096,3]{1,0:T(8,128)} reduce(f32[4096,1,3]{2,1,0:T(1,128)S(1)} %bitcast.337, f32[]{:T(128)} %broadcast.734), dimensions={1}, to_apply=%bitcast.275.reduce_sub_computation | reduce | bytes 98308
  285.8 19.4 %reduce.16 = f32[4096,3]{1,0:T(8,128)} reduce(f32[4096,1,3]{2,1,0:T(1,128)S(1)} %bitcast.338, f32[]{:T(128)} %broadcast.734), dimensions={1}, to_apply=%bitcast.279.reduce_sub_computation | reduce | bytes 98308
  309.0 6.9 %all-to-all-start.9 = ((f32[8,1,1536]{2,1,0:T(1,128)}), f32[8,1,1536]{2,1,0:T(1,128)S(1)}, u32[]{:S(2)}, u32[]{:S(2)}) async-start(f32[8,1,1536]{2,1,0:T(1,128)} %reshape.500), calls=%async_computation.9 | async-start | bytes 98304 | tf_op jit(solution)/shard_map/all_to_all | solution.py:203
  329.1 6.8 %all-to-all-start.8 = ((f32[32,1,384]{2,1,0:T(1,128)}), f32[32,1,384]{2,1,0:T(1,128)S(1)}, u32[]{:S(2)}, u32[]{:S(2)}) async-start(f32[32,1,384]{2,1,0:T(1,128)} %reshape.498), calls=%async_computation.8 | async-start | bytes 98304 | tf_op jit(solution)/shard_map/all_to_all | solution.py:212
  336.0 24.9 %all-reduce.2 = (f32[3,64,64]{2,1,0:T(8,128)S(1)}, f32[64,3]{0,1:T(4,128)S(1)}) all-reduce(f32[3,64,64]{2,1,0:T(8,128)S(1)} %pad_maximum_fusion.6, f32[64,3]{0,1:T(4,128)S(1)} %fusion.359), channel_id=1, replica_groups=mesh['rows'=8,'cols'=32] {'rows'}, use_global_device_ids=true, to_apply=%region_4.0 | all-reduce | flops 12480 | bytes 99840 | tf_op jit(solution)/shard_map/psum | solution.py:303
  360.8 125.9 %all-reduce = (f32[3,64,64]{2,1,0:T(8,128)S(1)}, f32[64,3]{0,1:T(4,128)S(1)}) all-reduce(f32[3,64,64]{2,1,0:T(8,128)S(1)} %get-tuple-element.9, f32[64,3]{0,1:T(4,128)S(1)} %get-tuple-element.10), channel_id=1, replica_groups=mesh['rows'=8,'cols'=32] {'cols'}, use_global_device_ids=true, to_apply=%region_5.0 | all-reduce | flops 12480 | bytes 99840 | tf_op jit(solution)/shard_map/psum | solution.py:302
  499.1 9.4 %all-to-all-start.10 = ((f32[32,1,384]{2,1,0:T(1,128)}), f32[32,1,384]{2,1,0:T(1,128)S(1)}, u32[]{:S(2)}, u32[]{:S(2)}) async-start(f32[32,1,384]{2,1,0:T(1,128)} %reshape.502), calls=%async_computation.10 | async-start | bytes 98304 | tf_op jit(solution)/shard_map/all_to_all | solution.py:219
  521.5 4.9 all-to-all-start.12
  528.0 5.6 all-to-all-done.12
  539.6 5.4 all-to-all-done.11
  551.6 99.3 %all-reduce.7.cloned.1.call-done = (f32[3,128,64]{1,2,0:T(8,128)}, f32[3,128,64]{1,2,0:T(8,128)}) async-done(((f32[3,128,64]{1,2,0:T(8,128)}, f32[3,128,64]{1,2,0:T(8,128)}), (f32[3,128,64]{1,2,0:T(8,128)}, f32[3,128,64]{1,2,0:T(8,128)})) %all-reduce.7.cloned.1.call-update) | async-done | bytes 196624 | tf_op jit(solution)/shard_map/psum | solution.py:302
  (279 shorter events, 195.1 us)
Async XLA Ops:
  9.2 37.3 %copy-start = (bf16[64,4096]{1,0:T(8,128)(2,1)}, bf16[64,4096]{1,0:T(8,128)(2,1)S(1)}, u32[]{:S(2)}) copy-start(bf16[64,4096]{1,0:T(8,128)(2,1)S(1)} %fusion.33) | copy-start | bytes 1572868
  9.9 36.6 %collective-permute-start = (bf16[64,256]{1,0:T(8,128)(2,1)}, bf16[64,256]{1,0:T(8,128)(2,1)}, u32[]{:S(2)}, u32[]{:S(2)}) collective-permute-start(bf16[64,256]{1,0:T(8,128)(2,1)} %slice.140), channel_id=1, source_target_pairs={{0,1},{1,2},{2,3},{3,4},{4,5},{5,6},{6,7},{7,8},{8,9},{9,10},{10,1... | collective-permute-start | bytes 98312 | tf_op jit(solution)/shard_map/ppermute | solution.py:13
  49.1 3.1 collective-permute-start.1
  53.5 5.1 collective-permute-start.2
  62.5 6.2 collective-permute-start.3
  71.4 5.6 collective-permute-start.4
  78.5 56.7 %copy-start.2 = (bf16[64,4096]{1,0:T(8,128)(2,1)}, bf16[64,4096]{1,0:T(8,128)(2,1)S(1)}, u32[]{:S(2)}) copy-start(bf16[64,4096]{1,0:T(8,128)(2,1)S(1)} %get-tuple-element.13) | copy-start | bytes 1572868
  78.8 5.6 collective-permute-start.5
  114.1 28.1 %all-to-all-start = ((f32[8,1,1536]{2,1,0:T(1,128)}), f32[8,1,1536]{2,1,0:T(1,128)S(1)}, u32[]{:S(2)}, u32[]{:S(2)}) async-start(f32[8,1,1536]{2,1,0:T(1,128)} %reshape.486), calls=%async_computation | async-start | bytes 98304 | tf_op jit(solution)/shard_map/all_to_all | solution.py:138
  159.5 21.8 %all-to-all-start.1 = ((f32[32,1,384]{2,1,0:T(1,128)}), f32[32,1,384]{2,1,0:T(1,128)S(1)}, u32[]{:S(2)}, u32[]{:S(2)}) async-start(f32[32,1,384]{2,1,0:T(1,128)} %reshape.488), calls=%async_computation.1 | async-start | bytes 98304 | tf_op jit(solution)/shard_map/all_to_all | solution.py:146
  181.3 14.1 %all-to-all-start.2 = ((f32[32,1,384]{2,1,0:T(1,128)}), f32[32,1,384]{2,1,0:T(1,128)S(1)}, u32[]{:S(2)}, u32[]{:S(2)}) async-start(f32[32,1,384]{2,1,0:T(1,128)} %reshape.490), calls=%async_computation.2 | async-start | bytes 98304 | tf_op jit(solution)/shard_map/all_to_all | solution.py:153
  203.5 12.2 %all-to-all-start.3 = ((f32[32,1,384]{2,1,0:T(1,128)}), f32[32,1,384]{2,1,0:T(1,128)S(1)}, u32[]{:S(2)}, u32[]{:S(2)}) async-start(f32[32,1,384]{2,1,0:T(1,128)} %reshape.492), calls=%async_computation.3 | async-start | bytes 98304 | tf_op jit(solution)/shard_map/all_to_all | solution.py:170
  215.7 11.3 %all-to-all-start.5 = ((f32[32,1,384]{2,1,0:T(1,128)}), f32[32,1,384]{2,1,0:T(1,128)S(1)}, u32[]{:S(2)}, u32[]{:S(2)}) async-start(f32[32,1,384]{2,1,0:T(1,128)} %reshape.494), calls=%async_computation.5 | async-start | bytes 98304 | tf_op jit(solution)/shard_map/all_to_all | solution.py:171
  227.0 10.4 %all-to-all-start.4 = ((f32[3,8,512]{2,0,1:T(4,128)}), f32[3,8,512]{2,0,1:T(4,128)S(1)}, u32[]{:S(2)}, u32[]{:S(2)}) async-start(f32[3,8,512]{2,0,1:T(4,128)} %reshape.475), calls=%async_computation.4 | async-start | bytes 131072 | tf_op jit(solution)/shard_map/all_to_all | solution.py:174
  230.3 307.9 %all-reduce.9.cloned.1.call-start = ((), (), s32[]{:S(2)}) async-start(), calls=%async_computation.15 | async-start | bytes 393216 | tf_op jit(solution)/shard_map/psum | solution.py:303
  237.4 10.7 %all-to-all-start.6 = ((f32[3,8,512]{2,0,1:T(4,128)}), f32[3,8,512]{2,0,1:T(4,128)S(1)}, u32[]{:S(2)}, u32[]{:S(2)}) async-start(f32[3,8,512]{2,0,1:T(4,128)} %reshape.476), calls=%async_computation.6 | async-start | bytes 131072 | tf_op jit(solution)/shard_map/all_to_all | solution.py:181
  279.7 29.2 %all-to-all-start.7 = ((f32[8,1,1536]{2,1,0:T(1,128)}), f32[8,1,1536]{2,1,0:T(1,128)S(1)}, u32[]{:S(2)}, u32[]{:S(2)}) async-start(f32[8,1,1536]{2,1,0:T(1,128)} %reshape.496), calls=%async_computation.7 | async-start | bytes 98304 | tf_op jit(solution)/shard_map/all_to_all | solution.py:196
  309.0 20.2 %all-to-all-start.9 = ((f32[8,1,1536]{2,1,0:T(1,128)}), f32[8,1,1536]{2,1,0:T(1,128)S(1)}, u32[]{:S(2)}, u32[]{:S(2)}) async-start(f32[8,1,1536]{2,1,0:T(1,128)} %reshape.500), calls=%async_computation.9 | async-start | bytes 98304 | tf_op jit(solution)/shard_map/all_to_all | solution.py:203
  329.1 169.9 %all-to-all-start.8 = ((f32[32,1,384]{2,1,0:T(1,128)}), f32[32,1,384]{2,1,0:T(1,128)S(1)}, u32[]{:S(2)}, u32[]{:S(2)}) async-start(f32[32,1,384]{2,1,0:T(1,128)} %reshape.498), calls=%async_computation.8 | async-start | bytes 98304 | tf_op jit(solution)/shard_map/all_to_all | solution.py:212
  499.1 16.7 %all-to-all-start.10 = ((f32[32,1,384]{2,1,0:T(1,128)}), f32[32,1,384]{2,1,0:T(1,128)S(1)}, u32[]{:S(2)}, u32[]{:S(2)}) async-start(f32[32,1,384]{2,1,0:T(1,128)} %reshape.502), calls=%async_computation.10 | async-start | bytes 98304 | tf_op jit(solution)/shard_map/all_to_all | solution.py:219
  521.5 12.2 %all-to-all-start.12 = ((f32[32,1,384]{2,1,0:T(1,128)}), f32[32,1,384]{2,1,0:T(1,128)S(1)}, u32[]{:S(2)}, u32[]{:S(2)}) async-start(f32[32,1,384]{2,1,0:T(1,128)} %reshape.506), calls=%async_computation.12 | async-start | bytes 98304 | tf_op jit(solution)/shard_map/all_to_all | solution.py:233
  533.7 11.3 %all-to-all-start.11 = ((f32[32,1,384]{2,1,0:T(1,128)}), f32[32,1,384]{2,1,0:T(1,128)S(1)}, u32[]{:S(2)}, u32[]{:S(2)}) async-start(f32[32,1,384]{2,1,0:T(1,128)} %reshape.504), calls=%async_computation.11 | async-start | bytes 98304 | tf_op jit(solution)/shard_map/all_to_all | solution.py:232
  537.6 113.3 %all-reduce.7.cloned.1.call-start = ((), (), s32[]{:S(2)}) async-start(), calls=%async_computation.14 | async-start | bytes 393216 | tf_op jit(solution)/shard_map/psum | solution.py:302
  547.4 105.1 %all-to-all-start.13 = ((f32[3,8,512]{2,0,1:T(4,128)}), f32[3,8,512]{2,0,1:T(4,128)S(1)}, u32[]{:S(2)}, u32[]{:S(2)}) async-start(f32[3,8,512]{2,0,1:T(4,128)} %copy.204), calls=%async_computation.13 | async-start | bytes 131072 | tf_op jit(solution)/shard_map/all_to_all | solution.py:241
  (36 other events, 351.6 us)
Sparse Core Ops, SparseCore 0:
  234.1 65.3 all-reduce.8
  541.8 109.0 all-reduce.6
